TPU v7x, 256 devices: a whole 4x4x8 slice. The times are simulated.
256 devices in a mesh: wide: 64 (over y, z, core), narrow: 4 (over x).
Axes of the slice: x: 4, y: 4, z: 8, core: 2. Of those that a mesh axis runs over, the one named last changes fastest.
Arguments:
- embedding: float32 [131072, 128], P(('wide', 'narrow'))
- tile_blocks: bfloat16 [64, 4, 22, 512, 512], P('wide', 'narrow'), may hold values from -0.125 to 0.125
- tile_row: int32 [64, 4, 22], P('wide', 'narrow'), may hold values from 0 to 3
- tile_col: int32 [64, 4, 22], P('wide', 'narrow'), may hold values from 0 to 63
- counts: int32 [64, 4], P('wide', 'narrow'), may hold values from 1 to 22, as said below
Outputs:
- orthonormal: float32 [131072, 128], P(('wide', 'narrow'))
Inputs may be any that keep to these rules, and one draw needn't show every extreme that they name: Slots 0 to counts[w, n] - 1 of device (w, n) hold its tiles, the others are unused; some device has all 22 slots live.
All inputs are finite; a program needn't handle non-finite values.
Results may differ from a plain program's by a relative error of at most 0.0036.
Values may be sent and summed in bfloat16 or wider, within the bound.
No kernel may reach another device: no remote copies, remote signals or barrier semaphores. Data moves between devices by JAX's collectives and lax.ppermute only.
A program may use at most 64 MiB of HBM per device.

v0:
```python
import jax
import jax.numpy as jnp
from jax import lax
from jax.sharding import PartitionSpec as P


def apply_operator(values_bf, tile_local, row_local, col_local, live_count):
    tile_size = tile_local.shape[1]
    width = values_bf.shape[1]
    rows_dev = values_bf.shape[0]
    slab_count = lax.axis_size("narrow") * rows_dev // tile_size
    slot_count = tile_local.shape[0]
    gathered = lax.all_gather(values_bf, "wide", axis=0, tiled=True)
    blocks = gathered.reshape(-1, tile_size, width)
    picked = jnp.take(blocks, col_local, axis=0)
    products = jnp.einsum("sij,sjk->sik", tile_local, picked, preferred_element_type=jnp.float32)
    slot_ids = jnp.arange(slot_count, dtype=jnp.int32)
    slab_ids = jnp.arange(slab_count, dtype=jnp.int32)
    onehot = ((row_local[None, :] == slab_ids[:, None]) & (slot_ids[None, :] < live_count)).astype(
        jnp.float32
    )
    partial_value = jnp.einsum("rs,sik->rik", onehot, products, precision=lax.Precision.HIGHEST)
    partial_value = partial_value.reshape(slab_count * tile_size, width)
    slab_total = lax.psum(partial_value, "narrow")
    return lax.dynamic_slice_in_dim(slab_total, lax.axis_index("narrow") * rows_dev, rows_dev, 0)


def local(embedding, tile_blocks, tile_row, tile_col, counts):
    tile_local = tile_blocks[0, 0]
    row_local = tile_row[0, 0]
    col_local = tile_col[0, 0]
    live_count = counts[0, 0]
    emb_bf = embedding.astype(jnp.bfloat16)
    first_order = apply_operator(emb_bf, tile_local, row_local, col_local, live_count)
    first_bf = first_order.astype(jnp.bfloat16)
    second = (
        2.0 * apply_operator(first_bf, tile_local, row_local, col_local, live_count) - embedding
    )
    spectral = 1.2661 * embedding - 1.1303 * first_order + 0.2715 * second
    gram_part = lax.dot_general(
        spectral, spectral, (((0,), (0,)), ((), ())), precision=lax.Precision.HIGHEST
    )
    gram_matrix = lax.psum(gram_part, ("wide", "narrow"))
    lower_factor = jnp.linalg.cholesky(gram_matrix)
    solved = jax.scipy.linalg.solve_triangular(lower_factor, spectral.T, lower=True)
    node_total = embedding.shape[0] * lax.axis_size("wide") * lax.axis_size("narrow")
    return solved.T * jnp.sqrt(jnp.float32(node_total))


def solution(mesh):
    placed = (
        P(("wide", "narrow"), None),
        P("wide", "narrow", None, None, None),
        P("wide", "narrow", None),
        P("wide", "narrow", None),
        P("wide", "narrow"),
    )
    return jax.shard_map(
        local, mesh=mesh, in_specs=placed, out_specs=P(("wide", "narrow"), None), check_vma=False
    )
```

profile of v0, /device:TPU:1, one launch (start us, length us, event | category | flops | bytes accessed | tf_op | source)
XLA Modules:
  0.0 617.0 jit_solution(5770539556316250015)
XLA Ops:
  6.5 0.0 all-gather.3.cloned.1.call-start
  6.5 1.6 convert_element_type.8
  8.2 0.0 all-gather.3.cloned.1.call-update
  8.2 0.0 all-reduce.4.cloned.1.call-start
  8.9 0.7 compare_select_fusion
  9.6 0.7 compare_and_fusion
  10.2 87.1 %all-gather.3.cloned.1.call-done = bf16[32768,128]{1,0:T(8,128)(2,1)} async-done(((bf16[512,128]{1,0:T(8,128)(2,1)}), bf16[32768,128]{1,0:T(8,128)(2,1)}) %all-gather.3.cloned.1.call-update) | async-done | bytes 8388624 | tf_op jit(solution)/shard_map/all_gather | solution.py:13
  97.3 4.5 gather_fusion
  101.8 11.3 %fusion.2 = f32[22,128,512]{2,1,0:T(8,128)} fusion(bf16[1,1,22,512,512]{4,3,2,1,0:T(8,128)(2,1)} %param.8, bf16[22,512,128]{2,1,0:T(8,128)(2,1)S(1)} %gather_fusion, pred[22]{0:T(512)(128)(4,1)S(1)} %compare_and_fusion), kind=kOutput, calls=%fused_computation.4 | convolution fusion | flops 1477836800 | bytes 20185110 | tf_op jit(solution)/shard_map/sij,sjk->sik/dot_general | solution.py:16
  113.1 0.0 copy-start.1
  113.1 6.5 %copy.12 = f32[22,128,512]{1,0,2:T(8,128)} copy(f32[22,128,512]{2,1,0:T(8,128)} %fusion.2) | data formatting | bytes 11534336 | tf_op jit(solution)/shard_map/sij,sjk->sik/dot_general | solution.py:16
  119.6 0.0 copy-done.1
  119.6 5.0 fusion.6
  124.6 1.0 copy.8
  125.6 0.0 all-reduce.4.cloned.1.call-update
  125.6 0.0 all-gather.5.cloned.1.call-start
  125.7 45.8 %all-reduce.4.cloned.1.call-done = f32[2048,128]{1,0:T(8,128)} async-done(((f32[2048,128]{1,0:T(8,128)}), f32[2048,128]{1,0:T(8,128)}) %all-reduce.4.cloned.1.call-update) | async-done | bytes 1048592 | tf_op jit(solution)/shard_map/psum | solution.py:24
  171.5 1.6 dynamic-slice_convert_fusion
  173.2 0.0 all-gather.5.cloned.1.call-update
  173.2 0.2 all-reduce.6.cloned.1.call-start
  173.4 87.1 %all-gather.5.cloned.1.call-done = bf16[32768,128]{1,0:T(8,128)(2,1)} async-done(((bf16[512,128]{1,0:T(8,128)(2,1)}), bf16[32768,128]{1,0:T(8,128)(2,1)}) %all-gather.5.cloned.1.call-update) | async-done | bytes 8388624 | tf_op jit(solution)/shard_map/all_gather | solution.py:13
  260.5 4.5 gather_fusion.1
  265.0 11.3 %fusion = f32[22,128,512]{2,1,0:T(8,128)} fusion(bf16[1,1,22,512,512]{4,3,2,1,0:T(8,128)(2,1)} %param.8, bf16[22,512,128]{2,1,0:T(8,128)(2,1)S(1)} %gather_fusion.1, pred[22]{0:T(512)(128)(4,1)S(1)} %compare_and_fusion), kind=kOutput, calls=%fused_computation.2 | convolution fusion | flops 1477836800 | bytes 20185110 | tf_op jit(solution)/shard_map/sij,sjk->sik/dot_general | solution.py:16
  276.3 6.4 %copy.13 = f32[22,128,512]{1,0,2:T(8,128)} copy(f32[22,128,512]{2,1,0:T(8,128)} %fusion) | data formatting | bytes 11534336 | tf_op jit(solution)/shard_map/sij,sjk->sik/dot_general | solution.py:16
  282.7 0.0 copy-start
  282.7 5.1 fusion.4
  287.8 1.1 copy.9
  288.9 0.0 all-reduce.6.cloned.1.call-update
  288.9 0.3 all-reduce.8.cloned.1.call-start
  289.2 45.6 %all-reduce.6.cloned.1.call-done = f32[2048,128]{1,0:T(8,128)} async-done(((f32[2048,128]{1,0:T(8,128)}), f32[2048,128]{1,0:T(8,128)}) %all-reduce.6.cloned.1.call-update) | async-done | bytes 1048592 | tf_op jit(solution)/shard_map/psum | solution.py:24
  334.8 0.0 copy-done
  334.8 1.1 multiply_add_fusion
  335.9 1.2 fusion.23
  337.1 0.0 all-reduce.8.cloned.1.call-update
  337.1 247.6 %all-reduce.8.cloned.1.call-done = f32[128,128]{0,1:T(8,128)} async-done(((f32[128,128]{0,1:T(8,128)}), f32[128,128]{0,1:T(8,128)}) %all-reduce.8.cloned.1.call-update) | async-done | bytes 65552 | tf_op jit(solution)/shard_map/psum | solution.py:43
  584.7 0.9 copy.11
  585.6 0.9 fusion.16
  586.5 11.7 %cholesky.16 = f32[128,128]{1,0:T(8,128)S(1)} custom-call(f32[128,128]{1,0:T(8,128)S(1)} %fusion.16), custom_call_target="Cholesky" | custom-call | tf_op jit(solution)/shard_map/jit(cholesky)/cholesky | solution.py:44
  598.2 0.6 compare_reduce_fusion
  598.9 0.7 fusion.14
  599.5 9.8 %custom-call.7 = f32[1,128,128]{1,2,0:T(8,128)S(1)} custom-call(f32[1,128,128]{2,1,0:T(8,128)S(1)} %fusion.14), custom_call_target="InvertDiagBlocksLowerTriangular" | custom-call | tf_op jit(solution)/shard_map/jit(_solve_triangular)/triangular_solve | solution.py:45
  609.4 1.1 convolution_multiply_fusion
  (3 shorter events, 0.1 us)
Async XLA Ops:
  6.5 90.8 %all-gather.3.cloned.1.call-start = ((), (), s32[]{:S(2)}) async-start(), calls=%async_computation | async-start | bytes 8519680 | tf_op jit(solution)/shard_map/all_gather | solution.py:13
  8.2 163.4 %all-reduce.4.cloned.1.call-start = ((), (), s32[]{:S(2)}) async-start(), calls=%async_computation.1 | async-start | bytes 2097152 | tf_op jit(solution)/shard_map/psum | solution.py:24
  113.1 6.5 %copy-start.1 = (s32[1,1,22]{2,1,0:T(1,128)S(1)}, s32[1,1,22]{2,1,0:T(1,128)}, u32[]{:S(2)}) copy-start(s32[1,1,22]{2,1,0:T(1,128)} %param.9) | copy-start | bytes 268
  125.6 134.9 %all-gather.5.cloned.1.call-start = ((), (), s32[]{:S(2)}) async-start(), calls=%async_computation.2 | async-start | bytes 8519680 | tf_op jit(solution)/shard_map/all_gather | solution.py:13
  173.2 161.6 %all-reduce.6.cloned.1.call-start = ((), (), s32[]{:S(2)}) async-start(), calls=%async_computation.3 | async-start | bytes 2097152 | tf_op jit(solution)/shard_map/psum | solution.py:24
  282.7 52.1 %copy-start = (f32[512,128]{1,0:T(8,128)S(1)}, f32[512,128]{1,0:T(8,128)}, u32[]{:S(2)}) copy-start(f32[512,128]{1,0:T(8,128)} %param.7) | copy-start | bytes 786436
  288.9 295.8 %all-reduce.8.cloned.1.call-start = ((), (), s32[]{:S(2)}) async-start(), calls=%async_computation.4 | async-start | bytes 131072 | tf_op jit(solution)/shard_map/psum | solution.py:43
Sparse Core Ops, SparseCore 0:
  10.1 87.1 all-gather.2
  125.8 45.7 all-reduce.3
  174.3 86.1 all-gather.4
  289.0 45.7 all-reduce.5
  340.1 244.5 all-reduce.7
where the time goes:
time: 618 us; the launch traced here: 617 us
  waiting for transfers between devices  513 us (83%)
  matrix products  34.9 us (6%)
  other arithmetic  27.8 us (4%)
  local copies, waits for them, and re-layouts  26.5 us (4%)
  between operations  13.9 us (2%)
    psum x1, waiting for transfers between devices, local(): gram_matrix = lax.psum(gram_part, ('wide', 'narrow'))  248 us
    all_gather x2, waiting for transfers between devices, apply_operator(): gathered = lax.all_gather(values_bf, 'wide', axis=0, tiled=True)  174 us
    psum x2, waiting for transfers between devices, apply_operator(): slab_total = lax.psum(partial_value, 'narrow')  91.4 us
    dot_general x2, matrix products, apply_operator(): jnp.einsum('sij,sjk->sik', tile_local, picked, preferred_element_type=jnp...  22.5 us
    dot_general x2, local copies, waits for them, and re-layouts, apply_operator(): jnp.einsum('sij,sjk->sik', tile_local, picked, preferred_element_type=jnp...  12.9 us
    another operation x3, other arithmetic, local(): lower_factor = jnp.linalg.cholesky(gram_matrix)  12.4 us
  transfers between devices with their start and end apart: 5, of which 5 were waited for; matrix products, arithmetic and copies ran while one was open for 0% of the time, Pallas kernels for 0%

commit v1 on v0

--- a/solution.py
+++ b/solution.py
@@ -10,7 +10,8 @@
     rows_dev = values_bf.shape[0]
     slab_count = lax.axis_size("narrow") * rows_dev // tile_size
     slot_count = tile_local.shape[0]
-    gathered = lax.all_gather(values_bf, "wide", axis=0, tiled=True)
+    sent = jnp.stack([values_bf] * lax.axis_size("wide"))
+    gathered = jnp.concatenate(lax.all_to_all(sent, "wide", 0, 0), axis=0)
     blocks = gathered.reshape(-1, tile_size, width)
     picked = jnp.take(blocks, col_local, axis=0)
     products = jnp.einsum("sij,sjk->sik", tile_local, picked, preferred_element_type=jnp.float32)

time: 618 us -> 845 us (1.37)
  blocking collectives: 0 us -> 198 us
  starting transfers between devices: 0.57 us -> 13.8 us
  waiting for transfers between devices: 513 us -> 524 us
    all_to_all x0 -> x1, blocking collectives: none -> 198 us  [apply_operator(): gathered = jnp.concatenate(lax.all_to_all(sent, 'wide', 0, 0), axis=0)]
    all_to_all x0 -> x1, waiting for transfers between devices: none -> 185 us  [apply_operator(): gathered = jnp.concatenate(lax.all_to_all(sent, 'wide', 0, 0), axis=0)]
    all_gather x2 -> x0, waiting for transfers between devices: 174 us -> none  [apply_operator(): gathered = lax.all_gather(values_bf, 'wide', axis=0, tiled=True)]
    all_to_all x0 -> x1, starting transfers between devices: none -> 13.5 us  [apply_operator(): gathered = jnp.concatenate(lax.all_to_all(sent, 'wide', 0, 0), axis=0)]
  transfers between devices with their start and end apart: 5 -> 4, of which waited for: 5 -> 4; matrix products, arithmetic and copies ran while one was open for 0% -> 0% of each run, Pallas kernels for 0% -> 0%
where the time goes in v1:
time: 845 us; the launch traced here: 844 us
  waiting for transfers between devices  524 us (62%)
  blocking collectives  198 us (23%)
  matrix products  34.9 us (4%)
  local copies, waits for them, and re-layouts  33.2 us (4%)
  other arithmetic  25.8 us (3%)
  between operations  13.9 us (2%)
  starting transfers between devices  13.8 us (2%)
    psum x1, waiting for transfers between devices, local(): gram_matrix = lax.psum(gram_part, ('wide', 'narrow'))  248 us
    all_to_all x1, blocking collectives, apply_operator(): gathered = jnp.concatenate(lax.all_to_all(sent, 'wide', 0, 0), axis=0)  198 us
    all_to_all x1, waiting for transfers between devices, apply_operator(): gathered = jnp.concatenate(lax.all_to_all(sent, 'wide', 0, 0), axis=0)  185 us
    psum x2, waiting for transfers between devices, apply_operator(): slab_total = lax.psum(partial_value, 'narrow')  91.4 us
    dot_general x2, matrix products, apply_operator(): jnp.einsum('sij,sjk->sik', tile_local, picked, preferred_element_type=jnp...  22.6 us
  transfers between devices with their start and end apart: 4, of which 4 were waited for; matrix products, arithmetic and copies ran while one was open for 0% of the time, Pallas kernels for 0%

profile of v1, /device:TPU:1, one launch (start us, length us, event | category | flops | bytes accessed | tf_op | source)
XLA Modules:
  0.0 844.1 jit_solution(16549925327088196718)
XLA Ops:
  6.5 1.0 convert_element_type.8
  7.5 5.2 stack.4
  12.7 0.0 copy-start.2
  12.7 13.5 %all-to-all-start = ((bf16[64,512,128]{2,1,0:T(8,128)(2,1)}), bf16[64,512,128]{2,1,0:T(8,128)(2,1)}, u32[]{:S(2)}, u32[]{:S(2)}) async-start(bf16[64,512,128]{2,1,0:T(8,128)(2,1)} %stack.4), calls=%async_computation | async-start | bytes 16777216 | tf_op jit(solution)/shard_map/all_to_all | solution.py:14
  26.2 0.0 all-reduce.4.cloned.1.call-start
  26.9 0.0 copy-done.2
  27.0 185.0 %all-to-all-done = bf16[64,512,128]{2,1,0:T(8,128)(2,1)} async-done(((bf16[64,512,128]{2,1,0:T(8,128)(2,1)}), bf16[64,512,128]{2,1,0:T(8,128)(2,1)}, u32[]{:S(2)}, u32[]{:S(2)}) %all-to-all-start) | async-done | bytes 8388640 | tf_op jit(solution)/shard_map/all_to_all | solution.py:14
  211.9 4.5 gather_fusion
  216.4 11.3 %fusion.2 = f32[22,128,512]{2,1,0:T(8,128)} fusion(bf16[1,1,22,512,512]{4,3,2,1,0:T(8,128)(2,1)} %param.8, bf16[22,512,128]{2,1,0:T(8,128)(2,1)S(1)} %gather_fusion, pred[22]{0:T(512)(128)(4,1)S(1)} %compare_and_fusion), kind=kOutput, calls=%fused_computation.4 | convolution fusion | flops 1477836800 | bytes 20185110 | tf_op jit(solution)/shard_map/sij,sjk->sik/dot_general | solution.py:17
  227.7 0.0 copy-start.1
  227.7 6.5 copy.12
  234.2 0.0 copy-done.1
  234.2 5.0 fusion.6
  239.2 1.1 copy.8
  240.3 0.0 all-reduce.4.cloned.1.call-update
  240.3 0.0 all-reduce.6.cloned.1.call-start
  240.4 46.0 %all-reduce.4.cloned.1.call-done = f32[2048,128]{1,0:T(8,128)} async-done(((f32[2048,128]{1,0:T(8,128)}), f32[2048,128]{1,0:T(8,128)}) %all-reduce.4.cloned.1.call-update) | async-done | bytes 1048592 | tf_op jit(solution)/shard_map/psum | solution.py:25
  286.3 1.0 dynamic-slice_convert_fusion
  287.3 2.0 stack.5
  289.3 198.4 %all_to_all.10 = bf16[64,512,128]{2,1,0:T(8,128)(2,1)} all-to-all(bf16[64,512,128]{2,1,0:T(8,128)(2,1)S(1)} %stack.5), channel_id=1, replica_groups=mesh['wide'=64,'narrow'=4] {'wide'}, dimensions={0} | all-to-all | bytes 16777216 | tf_op jit(solution)/shard_map/all_to_all | solution.py:14
  487.7 4.5 gather_fusion.1
  492.2 11.3 %fusion = f32[22,128,512]{2,1,0:T(8,128)} fusion(bf16[1,1,22,512,512]{4,3,2,1,0:T(8,128)(2,1)} %param.8, bf16[22,512,128]{2,1,0:T(8,128)(2,1)S(1)} %gather_fusion.1, pred[22]{0:T(512)(128)(4,1)S(1)} %compare_and_fusion), kind=kOutput, calls=%fused_computation.2 | convolution fusion | flops 1477836800 | bytes 20185110 | tf_op jit(solution)/shard_map/sij,sjk->sik/dot_general | solution.py:17
  503.5 6.5 copy.13
  510.0 0.0 copy-start
  510.0 5.1 fusion.4
  515.0 1.1 copy.9
  516.1 0.0 all-reduce.6.cloned.1.call-update
  516.2 0.3 all-reduce.8.cloned.1.call-start
  516.4 45.4 %all-reduce.6.cloned.1.call-done = f32[2048,128]{1,0:T(8,128)} async-done(((f32[2048,128]{1,0:T(8,128)}), f32[2048,128]{1,0:T(8,128)}) %all-reduce.6.cloned.1.call-update) | async-done | bytes 1048592 | tf_op jit(solution)/shard_map/psum | solution.py:25
  561.8 0.0 copy-done
  561.8 1.1 multiply_add_fusion
  562.9 1.2 fusion.23
  564.1 0.0 all-reduce.8.cloned.1.call-update
  564.2 247.7 %all-reduce.8.cloned.1.call-done = f32[128,128]{0,1:T(8,128)} async-done(((f32[128,128]{0,1:T(8,128)}), f32[128,128]{0,1:T(8,128)}) %all-reduce.8.cloned.1.call-update) | async-done | bytes 65552 | tf_op jit(solution)/shard_map/psum | solution.py:44
  811.8 0.9 copy.11
  812.8 0.9 fusion.16
  813.6 11.7 %cholesky.16 = f32[128,128]{1,0:T(8,128)S(1)} custom-call(f32[128,128]{1,0:T(8,128)S(1)} %fusion.16), custom_call_target="Cholesky" | custom-call | tf_op jit(solution)/shard_map/jit(cholesky)/cholesky | solution.py:45
  825.4 0.6 compare_reduce_fusion
  826.0 0.7 fusion.14
  826.7 9.8 %custom-call.7 = f32[1,128,128]{1,2,0:T(8,128)S(1)} custom-call(f32[1,128,128]{2,1,0:T(8,128)S(1)} %fusion.14), custom_call_target="InvertDiagBlocksLowerTriangular" | custom-call | tf_op jit(solution)/shard_map/jit(_solve_triangular)/triangular_solve | solution.py:46
  836.5 1.1 convolution_multiply_fusion
  (5 shorter events, 0.1 us)
Async XLA Ops:
  12.7 14.2 %copy-start.2 = (s32[1,1,22]{2,1,0:T(1,128)S(1)}, s32[1,1,22]{2,1,0:T(1,128)}, u32[]{:S(2)}) copy-start(s32[1,1,22]{2,1,0:T(1,128)} %param.10) | copy-start | bytes 268
  12.7 199.2 %all-to-all-start = ((bf16[64,512,128]{2,1,0:T(8,128)(2,1)}), bf16[64,512,128]{2,1,0:T(8,128)(2,1)}, u32[]{:S(2)}, u32[]{:S(2)}) async-start(bf16[64,512,128]{2,1,0:T(8,128)(2,1)} %stack.4), calls=%async_computation | async-start | bytes 16777216 | tf_op jit(solution)/shard_map/all_to_all | solution.py:14
  26.2 260.1 %all-reduce.4.cloned.1.call-start = ((), (), s32[]{:S(2)}) async-start(), calls=%async_computation.2 | async-start | bytes 2097152 | tf_op jit(solution)/shard_map/psum | solution.py:25
  227.7 6.5 copy-start.1
  240.3 321.5 %all-reduce.6.cloned.1.call-start = ((), (), s32[]{:S(2)}) async-start(), calls=%async_computation.3 | async-start | bytes 2097152 | tf_op jit(solution)/shard_map/psum | solution.py:25
  510.0 51.8 %copy-start = (f32[512,128]{1,0:T(8,128)S(1)}, f32[512,128]{1,0:T(8,128)}, u32[]{:S(2)}) copy-start(f32[512,128]{1,0:T(8,128)} %param.7) | copy-start | bytes 786436
  516.2 295.7 %all-reduce.8.cloned.1.call-start = ((), (), s32[]{:S(2)}) async-start(), calls=%async_computation.4 | async-start | bytes 131072 | tf_op jit(solution)/shard_map/psum | solution.py:44
Sparse Core Ops, SparseCore 0:
  240.4 45.8 all-reduce.3
  516.3 45.4 all-reduce.5
  567.3 244.4 all-reduce.7
